TPU v7x, 32 devices: a whole 2x2x4 slice. The times are simulated.
32 devices in a mesh: species: 4 (over z), wave: 8 (over y, x, core).
Axes of the slice: x: 2, y: 2, z: 4, core: 2. Of those that a mesh axis runs over, the one named last changes fastest.
Arguments:
- dest_tiles: int32 [4, 256, 1], P('species', 'wave'), may hold values from 0 to 7; in each aligned block of 32 rows (0 to 31, 32 to 63, ..., all dimensions but the last counted through in order) at most 8 rows name the same one
- line_counts: int32 [4, 256], P('species', 'wave'), may hold values from 32 to 128
- wing_widths: int32 [4, 256], P('species', 'wave'), may hold values from 16 to 64
- species_ids: int32 [4, 32768], P('species', 'wave'), may hold values from 0 to 3
- offsets: float32 [4, 32768], P('species', 'wave'), may hold values from 0 to 256
- strengths: float32 [4, 32768], P('species', 'wave'), may hold values from 0.01 to 0.2
- doppler: float32 [4, 32768], P('species', 'wave'), may hold values from 0.5 to 6
- lorentz: float32 [4, 32768], P('species', 'wave'), may hold values from 0.1 to 4
- energy: float32 [4, 32768], P('species', 'wave'), may hold values from 0.05 to 3
- temp_scale: float32 [16], replicated, may hold values from 0.5 to 2
- press_scale: float32 [16], replicated, may hold values from 0.2 to 4
- inverse_temp: float32 [16], replicated, may hold values from 0.2 to 1.5
- abundances: float32 [4, 4, 4, 16], P(None, 'species'), may hold values from 0.05 to 1
Outputs:
- opacity: float32 [4, 16, 2048], P(None, 'species', 'wave')
Inputs may be any that keep to these rules, and one draw needn't show every extreme that they name: `dest_tiles`: within one device's 32 blocks no tile is named more than 8 times.
All inputs are finite; a program needn't handle non-finite values.
Results may differ from a plain program's by a relative error of at most 0.0004.
Values sent between devices are 32-bit elements; how exact they have to be, the bound alone decides.
A program may use at most 64 MiB of HBM per device.

v0:
```python
import functools

import jax
import jax.numpy as jnp
from jax import lax
from jax.experimental import pallas as pl
from jax.experimental.pallas import tpu as pltpu
from jax.sharding import PartitionSpec as P

LANES = 128
HALO = 64
STEP = 16
WINDOW = LANES + STEP
SPAN = LANES + 2 * HALO
SHIFTS = LANES // STEP
FAR = 1e37
MESH = pl.DeviceIdType.MESH


def column(ref, count):
    rows = lax.broadcasted_iota(jnp.int32, (count, LANES), 0)
    out = jnp.zeros((count, LANES), jnp.float32)
    for index in range(count):
        out = jnp.where(rows == index, ref[index], out)
    return out


def kernel(
    sizes,
    tiles,
    counts,
    wings,
    temp,
    press,
    inverse,
    abund,
    kinds,
    offsets,
    strengths,
    doppler,
    lorentz,
    energy,
    out,
    square,
    decay,
    lor_amp,
    gau_amp,
    table,
    bits,
    route,
    coef,
    accum,
    send,
    recv,
    send_sem,
    recv_sem,
):
    nspecies, nwave, nblocks, points, mixes, sub, batch = sizes
    chunk = points // nspecies
    rows = 2 * mixes
    total_rows = nwave * rows
    me_s = lax.axis_index("species")
    me_w = lax.axis_index("wave")
    me = me_s * nwave + me_w
    count = nspecies * nwave

    barrier = pltpu.get_barrier_semaphore()

    def greet(step, carry):
        other = lax.rem(me + step, count)
        pl.semaphore_signal(
            barrier,
            inc=1,
            device_id=(lax.div(other, nwave), lax.rem(other, nwave)),
            device_id_type=MESH,
        )
        return carry

    lax.fori_loop(1, count, greet, 0)

    temp_col = column(temp, points)
    press_col = column(press, points)
    inverse_col = column(inverse, points)
    lane_row = lax.broadcasted_iota(jnp.int32, (1, LANES), 1)
    local = lax.broadcasted_iota(jnp.int32, (WINDOW, LANES), 0).astype(jnp.float32) - HALO
    row_point = lax.broadcasted_iota(jnp.int32, (points, LANES), 0)
    row8 = lax.broadcasted_iota(jnp.int32, (rows, LANES), 0)
    row_half = lax.div(row8, mixes)
    for mix in range(mixes):
        for kind in range(sub):
            value = jnp.zeros((points, LANES), jnp.float32)
            for point in range(points):
                value = jnp.where(row_point == point, abund[mix, 0, kind, point], value)
            coef[mix, kind] = value

    def prepare(block, carry):
        here = pl.ds(pl.multiple_of(block * LANES, LANES), LANES)
        center = offsets[:, here]
        upper = jnp.where(center >= float(LANES), 1.0, 0.0)
        center = center - upper * float(LANES)
        hop = jnp.clip(jnp.floor(center * (1.0 / STEP)), 0.0, float(SHIFTS - 1))
        reach = wings[0, block].astype(jnp.float32)
        offset = (local + hop * float(STEP)) - center
        sq = offset * offset
        square[:, here] = jnp.where(sq <= reach * reach, sq, FAR)
        hop_int = hop.astype(jnp.int32)
        for stage in range(3):
            bit = (hop_int >> stage) & 1
            bits[block, stage] = jnp.broadcast_to(bit.astype(jnp.float32), (STEP, LANES))
        gauss = 2.35482 * (temp_col * doppler[:, here])
        lor = 2.0 * (press_col * lorentz[:, here])
        g2 = gauss * gauss
        g4 = g2 * g2
        l2 = lor * lor
        l4 = l2 * l2
        poly = (
            g4 * gauss
            + 2.69269 * g4 * lor
            + 2.42843 * (g2 * gauss) * l2
            + 4.47163 * g2 * (l2 * lor)
            + 0.07842 * gauss * l4
            + l4 * lor
        )
        width = jnp.exp(0.2 * jnp.log(poly))
        inv = 1.0 / width
        ratio = lor * inv
        eta = ratio * (1.36603 + ratio * (-0.47719 + ratio * 0.11116))
        decay[block] = -4.0 * (inv * inv)
        lor_amp[block] = eta * inv * (4.0 * 0.15915494)
        gau_amp[block] = (1.0 - eta) * inv * 0.9394373
        boltz = jnp.exp(-(inverse_col * energy[:, here]))
        strength = jnp.where(lane_row < counts[0, block], strengths[:, here], 0.0)
        kind_row = kinds[:, here]
        for mix in range(mixes):
            mixed = coef[mix, 0]
            for kind in range(1, sub):
                mixed = jnp.where(kind_row == kind, coef[mix, kind], mixed)
            mixed = (mixed * strength) * boltz
            for half in range(2):
                table[block, pl.ds(half * mixes + mix, points, stride=rows), :] = mixed
        chosen = jnp.where(row_half.astype(jnp.float32) == upper, 1.0, 0.0)
        target = tiles[0, block]
        for tile in range(0, nwave, 2):
            pair = jnp.concatenate(
                [jnp.where(target == tile, chosen, 0.0), jnp.where(target == tile + 1, chosen, 0.0)],
                axis=0,
            )
            route[block, pl.ds(tile * rows, 2 * rows), :] = pair.astype(jnp.bfloat16)
        return carry

    lax.fori_loop(0, nblocks, prepare, 0, unroll=4)

    edge = jnp.zeros((8, SPAN), jnp.float32)
    accum[0:8, :] = edge
    accum[8 + total_rows :, :] = edge
    lane_full = lax.broadcasted_iota(jnp.int32, (total_rows, LANES), 1)

    def group_of(phase):
        return lax.rem(me_s + 1 + phase, nspecies)

    def evaluate(step, carry):
        group = group_of(lax.div(step, chunk))
        inner = lax.rem(step, chunk)
        point = group * chunk + inner
        accum[8 : 8 + total_rows, :] = jnp.zeros((total_rows, SPAN), jnp.float32)

        def blocks(part, carry):
            base = part * batch
            weights = []
            profiles = []
            for pair_index in range(batch // 2):
                halves = []
                for index in (2 * pair_index, 2 * pair_index + 1):
                    block = base + index
                    here = pl.ds(pl.multiple_of(block * LANES, LANES), LANES)
                    slope = jnp.broadcast_to(decay[block, pl.ds(point, 1), :], (STEP, LANES))
                    amp_l = jnp.broadcast_to(lor_amp[block, pl.ds(point, 1), :], (STEP, LANES))
                    amp_g = jnp.broadcast_to(gau_amp[block, pl.ds(point, 1), :], (STEP, LANES))
                    pieces = []
                    for piece in range(WINDOW // STEP):
                        sq = square[piece * STEP : (piece + 1) * STEP, here]
                        power = sq * slope
                        value = amp_l / (1.0 - power) + amp_g * jnp.exp2(power)
                        pieces.append(value.astype(jnp.bfloat16))
                    blank = jnp.zeros((STEP, LANES), jnp.bfloat16)
                    for stage in range(3):
                        hop = 1 << stage
                        on = bits[block, stage] > 0
                        shifted = [blank] * hop + pieces
                        stay = pieces + [blank] * hop
                        pieces = [jnp.where(on, a, b) for a, b in zip(shifted, stay)]
                    halves.append(jnp.concatenate(pieces, axis=0))
                    weight = table[block, pl.ds(pl.multiple_of(point * rows, rows), rows), :]
                    packed = jnp.concatenate([weight, weight], axis=0).astype(jnp.bfloat16)
                    weights.append(
                        jnp.concatenate(
                            [
                                packed * route[block, pair * 2 * rows : (pair + 1) * 2 * rows, :]
                                for pair in range(nwave // 2)
                            ],
                            axis=0,
                        )
                    )
                profiles.append(jnp.concatenate(halves, axis=1))
            weight = jnp.concatenate(weights, axis=1)
            accum[8 : 8 + total_rows, :] += lax.dot_general(
                weight,
                jnp.concatenate(profiles, axis=1),
                (((1,), (1,)), ((), ())),
                preferred_element_type=jnp.float32,
            )
            return carry

        lax.fori_loop(0, nblocks // batch, blocks, 0)
        low = accum[8 : 8 + total_rows, 0:LANES]
        high = accum[8 : 8 + total_rows, LANES:SPAN]
        high_prev = accum[8 - mixes : 8 - mixes + total_rows, LANES:SPAN]
        low_next = accum[8 + mixes : 8 + mixes + total_rows, 0:LANES]
        joined = jnp.where(lane_full >= HALO, low + high_prev, high + low_next)
        joined = pltpu.roll(joined, HALO, 1)
        for tile in range(nwave):
            send[group, tile, inner] = joined[tile * rows : (tile + 1) * rows]
        return carry

    def copy_to(group, tile):
        other = group * nwave + tile
        return pltpu.make_async_remote_copy(
            src_ref=send.at[group, tile],
            dst_ref=recv.at[me],
            send_sem=send_sem.at[other],
            recv_sem=recv_sem.at[me],
            device_id=(group, tile),
            device_id_type=MESH,
        )

    def start_phase(phase):
        group = group_of(phase)

        def start(step, carry):
            copy_to(group, lax.rem(me_w + step, nwave)).start()
            return carry

        lax.fori_loop(1 if phase == nspecies - 1 else 0, nwave, start, 0)

    done = 0
    for phase in range(nspecies):
        until = min((phase + 1) * chunk + 1, points)
        lax.fori_loop(done, until, evaluate, 0)
        done = until
        if phase == 0:
            pl.semaphore_wait(barrier, count - 1)
        start_phase(phase)

    def finish(step, carry):
        other = lax.rem(me + step, count)
        copy_to(lax.div(other, nwave), lax.rem(other, nwave)).wait_send()
        return carry

    lax.fori_loop(1, count, finish, 0)

    def gather(step, total):
        other = lax.rem(me + step, count)
        pltpu.make_async_remote_copy(
            src_ref=send.at[me_s, me_w],
            dst_ref=recv.at[other],
            send_sem=send_sem.at[other],
            recv_sem=recv_sem.at[other],
            device_id=(lax.div(other, nwave), lax.rem(other, nwave)),
            device_id_type=MESH,
        ).wait_recv()
        return total + recv[other]

    total = lax.fori_loop(1, count, gather, send[me_s, me_w])
    for mix in range(mixes):
        for half in range(2):
            out[mix, :, half * LANES : (half + 1) * LANES] = total[:, half * mixes + mix, :]


def per_device(
    dest_tiles,
    line_counts,
    wing_widths,
    species_ids,
    offsets,
    strengths,
    doppler,
    lorentz,
    energy,
    temp_scale,
    press_scale,
    inverse_temp,
    abundances,
):
    nspecies = lax.axis_size("species")
    nwave = lax.axis_size("wave")
    nblocks = dest_tiles.shape[1]
    mixes, _, sub, points = abundances.shape
    chunk = points // nspecies
    rows = 2 * mixes
    batch = 32
    lines = nblocks * LANES
    sizes = (nspecies, nwave, nblocks, points, mixes, sub, batch)
    smem = pl.BlockSpec(memory_space=pltpu.SMEM)
    vmem = pl.BlockSpec(memory_space=pltpu.VMEM)
    table = pltpu.VMEM((nblocks, points, LANES), jnp.float32)
    return pl.pallas_call(
        functools.partial(kernel, sizes),
        out_shape=jax.ShapeDtypeStruct((mixes, chunk, 2 * LANES), jnp.float32),
        in_specs=[smem] * 7 + [vmem] * 6,
        out_specs=vmem,
        scratch_shapes=[
            pltpu.VMEM((WINDOW, lines), jnp.float32),
            table,
            table,
            table,
            pltpu.VMEM((nblocks, points * rows, LANES), jnp.float32),
            pltpu.VMEM((nblocks, 3, STEP, LANES), jnp.float32),
            pltpu.VMEM((nblocks, nwave * rows, LANES), jnp.bfloat16),
            pltpu.VMEM((mixes, sub, points, LANES), jnp.float32),
            pltpu.VMEM((nwave * rows + 16, SPAN), jnp.float32),
            pltpu.VMEM((nspecies, nwave, chunk, rows, LANES), jnp.float32),
            pltpu.VMEM((nspecies * nwave, chunk, rows, LANES), jnp.float32),
            pltpu.SemaphoreType.DMA((nspecies * nwave,)),
            pltpu.SemaphoreType.DMA((nspecies * nwave,)),
        ],
        compiler_params=pltpu.CompilerParams(collective_id=0, has_side_effects=True),
    )(
        dest_tiles.reshape(1, nblocks),
        line_counts,
        wing_widths,
        temp_scale,
        press_scale,
        inverse_temp,
        abundances,
        species_ids,
        offsets,
        strengths,
        doppler,
        lorentz,
        energy,
    )


def solution(mesh):
    lines = P("species", "wave")
    return jax.shard_map(
        per_device,
        mesh=mesh,
        in_specs=(P("species", "wave", None),)
        + (lines,) * 8
        + (P(), P(), P(), P(None, "species", None, None)),
        out_specs=P(None, "species", "wave"),
        check_vma=False,
    )
```

profile of v0, /device:TPU:0, one launch (start us, length us, event | category | flops | bytes accessed | tf_op | source)
XLA Modules:
  0.0 31.0 jit_solution(7246183153635024952)
XLA Ops:
  0.0 29.7 %shard_map.127 = f32[4,4,256]{2,1,0:T(4,128)} custom-call(s32[1,32]{1,0:T(1,128)} %bitcast.1, s32[1,32]{1,0:T(1,128)} %counts.1, s32[1,32]{1,0:T(1,128)} %wings.1, f32[16]{0:T(128)} %temp.1, f32[16]{0:T(128)} %press.1, f32[16]{0:T(128)} %inverse.1, f32[4,1,4,16]{3,2,1,0:T(4,128)} %abund.1, s32[1,4096]{1,0:T(1,128)} %kinds.1, f32[1,4096]{1,0:T(1,128)} %offsets.1, ...), custom_call_target="tpu_custom_call" | custom-call | tf_op jit(solution)/shard_map/pallas_call | solution.py:306
  29.7 1.3 %copy.15 = f32[4,4,256]{2,1,0:T(4,128)} copy(f32[4,4,256]{2,1,0:T(4,128)} %shard_map.127) | data formatting | bytes 32768
where the time goes:
time: 31.3 us; the launch traced here: 31 us
  Pallas kernels  29.7 us (95%)
  local copies, waits for them, and re-layouts  1.32 us (4%)
    pallas_call x1, Pallas kernels, per_device(): pl.pallas_call(functools.partial(kernel, sizes), out_shape=jax.ShapeDtype...  29.7 us
    unnamed x1, local copies, waits for them, and re-layouts  1.32 us

commit v1 on v0

v1 whole, which is shorter than its diff:
```python
import functools

import jax
import jax.numpy as jnp
from jax import lax
from jax.experimental import pallas as pl
from jax.experimental.pallas import tpu as pltpu
from jax.sharding import PartitionSpec as P

LANES = 128
HALO = 64
STEP = 16
WINDOW = LANES + STEP
QUARTER = 64
SPAN = QUARTER + 2 * HALO
STAGES = 2
FAR = 1e37
MESH = pl.DeviceIdType.MESH


def column(ref, count):
    rows = lax.broadcasted_iota(jnp.int32, (count, LANES), 0)
    out = jnp.zeros((count, LANES), jnp.float32)
    for index in range(count):
        out = jnp.where(rows == index, ref[index], out)
    return out


def kernel(
    sizes,
    tiles,
    counts,
    wings,
    temp,
    press,
    inverse,
    abund,
    kinds,
    offsets,
    strengths,
    doppler,
    lorentz,
    energy,
    out,
    square,
    decay,
    lor_amp,
    gau_amp,
    table,
    bits,
    route,
    coef,
    accum,
    edge,
    send,
    recv,
    zsend,
    zrecv,
    send_sem,
    recv_sem,
    zsend_sem,
    zrecv_sem,
):
    nspecies, nwave, nblocks, points, mixes, sub = sizes
    chunk = points // nspecies
    last = nspecies - 1
    rows = 2 * mixes
    total_rows = nwave * rows
    me_s = lax.axis_index("species")
    me_w = lax.axis_index("wave")

    barrier = pltpu.get_barrier_semaphore()
    for step in range(1, nwave):
        pl.semaphore_signal(
            barrier,
            inc=1,
            device_id=(me_s, lax.rem(me_w + step, nwave)),
            device_id_type=MESH,
        )
    for step in range(1, nspecies):
        pl.semaphore_signal(
            barrier,
            inc=1,
            device_id=(lax.rem(me_s + step, nspecies), me_w),
            device_id_type=MESH,
        )

    temp_col = column(temp, points)
    press_col = column(press, points)
    inverse_col = column(inverse, points)
    lane_row = lax.broadcasted_iota(jnp.int32, (1, LANES), 1)
    local = lax.broadcasted_iota(jnp.int32, (WINDOW, LANES), 0).astype(jnp.float32) - HALO
    row_point = lax.broadcasted_iota(jnp.int32, (points, LANES), 0)
    row8 = lax.broadcasted_iota(jnp.int32, (rows, LANES), 0)
    row_half = lax.div(row8, mixes)
    for mix in range(mixes):
        for kind in range(sub):
            value = jnp.zeros((points, LANES), jnp.float32)
            for point in range(points):
                value = jnp.where(row_point == point, abund[mix, 0, kind, point], value)
            coef[mix, kind] = value

    def prepare(block, carry):
        here = pl.ds(pl.multiple_of(block * LANES, LANES), LANES)
        center = offsets[:, here]
        quarter = jnp.clip(jnp.floor(center * (1.0 / QUARTER)), 0.0, 3.0)
        center = center - quarter * float(QUARTER)
        hop = jnp.clip(jnp.floor(center * (1.0 / STEP)), 0.0, float(QUARTER // STEP - 1))
        reach = wings[0, block].astype(jnp.float32)
        offset = (local + hop * float(STEP)) - center
        sq = offset * offset
        square[:, here] = jnp.where(sq <= reach * reach, sq, FAR)
        hop_int = hop.astype(jnp.int32)
        for stage in range(STAGES):
            bit = (hop_int >> stage) & 1
            bits[block, stage] = jnp.broadcast_to(bit.astype(jnp.float32), (STEP, LANES))
        gauss = 2.35482 * (temp_col * doppler[:, here])
        lor = 2.0 * (press_col * lorentz[:, here])
        g2 = gauss * gauss
        g4 = g2 * g2
        l2 = lor * lor
        l4 = l2 * l2
        poly = (
            g4 * gauss
            + 2.69269 * g4 * lor
            + 2.42843 * (g2 * gauss) * l2
            + 4.47163 * g2 * (l2 * lor)
            + 0.07842 * gauss * l4
            + l4 * lor
        )
        width = jnp.exp(0.2 * jnp.log(poly))
        inv = 1.0 / width
        ratio = lor * inv
        eta = ratio * (1.36603 + ratio * (-0.47719 + ratio * 0.11116))
        decay[block] = -4.0 * (inv * inv)
        lor_amp[block] = eta * inv * (4.0 * 0.15915494)
        gau_amp[block] = (1.0 - eta) * inv * 0.9394373
        boltz = jnp.exp(-(inverse_col * energy[:, here]))
        strength = jnp.where(lane_row < counts[0, block], strengths[:, here], 0.0)
        kind_row = kinds[:, here]
        for mix in range(mixes):
            mixed = coef[mix, 0]
            for kind in range(1, sub):
                mixed = jnp.where(kind_row == kind, coef[mix, kind], mixed)
            mixed = (mixed * strength) * boltz
            for half in range(2):
                table[block, pl.ds(half * mixes + mix, points, stride=rows), :] = mixed
        target = tiles[0, block]
        for parity in range(2):
            chosen = jnp.where((2 * row_half + parity).astype(jnp.float32) == quarter, 1.0, 0.0)
            for tile in range(0, nwave, 2):
                pair = jnp.concatenate(
                    [jnp.where(target == tile, chosen, 0.0), jnp.where(target == tile + 1, chosen, 0.0)],
                    axis=0,
                )
                route[block, pl.ds(parity * total_rows + tile * rows, 2 * rows), :] = pair.astype(jnp.bfloat16)
        return carry

    lax.fori_loop(0, nblocks, prepare, 0, unroll=4)

    accum[...] = jnp.zeros(accum.shape, jnp.float32)
    edge[...] = jnp.zeros(edge.shape, jnp.float32)
    low_lane = lax.broadcasted_iota(jnp.int32, (total_rows, LANES), 1) < QUARTER

    def group_of(phase):
        return lax.rem(me_s + 1 + phase, nspecies)

    def evaluate(phase, inner):
        point = group_of(phase) * chunk + inner
        weights = []
        profiles = []
        for block in range(nblocks):
            here = pl.ds(block * LANES, LANES)
            slope = jnp.broadcast_to(decay[block, pl.ds(point, 1), :], (STEP, LANES))
            amp_l = jnp.broadcast_to(lor_amp[block, pl.ds(point, 1), :], (STEP, LANES))
            amp_g = jnp.broadcast_to(gau_amp[block, pl.ds(point, 1), :], (STEP, LANES))
            pieces = []
            for piece in range(WINDOW // STEP):
                sq = square[piece * STEP : (piece + 1) * STEP, here]
                power = sq * slope
                value = amp_l / (1.0 - power) + amp_g * jnp.exp2(power)
                pieces.append(value.astype(jnp.bfloat16))
            blank = jnp.zeros((STEP, LANES), jnp.bfloat16)
            for stage in range(STAGES):
                hop = 1 << stage
                on = bits[block, stage] > 0
                shifted = [blank] * hop + pieces
                stay = pieces + [blank] * hop
                pieces = [jnp.where(on, a, b) for a, b in zip(shifted, stay)]
            profiles.append(jnp.concatenate(pieces, axis=0))
            weight = table[block, pl.ds(pl.multiple_of(point * rows, rows), rows), :]
            packed = jnp.concatenate([weight, weight], axis=0).astype(jnp.bfloat16)
            weights.append(
                jnp.concatenate(
                    [
                        packed * route[block, part * 2 * rows : (part + 1) * 2 * rows, :]
                        for part in range(nwave)
                    ],
                    axis=0,
                )
            )
        accum[:, 0:SPAN] = lax.dot_general(
            jnp.concatenate(weights, axis=1),
            jnp.concatenate(profiles, axis=1),
            (((1,), (1,)), ((), ())),
            preferred_element_type=jnp.float32,
        )
        even_a = pltpu.roll(accum[0:total_rows, 0:LANES], QUARTER, 1)
        even_b = pltpu.roll(accum[0:total_rows, LANES : 2 * LANES], QUARTER, 1)
        odd_a = accum[total_rows : 2 * total_rows, 0:LANES]
        odd_b = accum[total_rows : 2 * total_rows, LANES : 2 * LANES]
        edge[rows : rows + total_rows, :] = jnp.where(low_lane, odd_b, even_a)
        above = edge[rows - mixes : rows - mixes + total_rows, :]
        below = edge[rows + mixes : rows + mixes + total_rows, :]
        joined = (odd_a + jnp.where(low_lane, even_a, even_b)) + jnp.where(low_lane, above, below)
        for tile in range(nwave):
            send[phase, tile, inner] = joined[tile * rows : (tile + 1) * rows]

    def plane_copy(phase, step):
        other = lax.rem(me_w + step, nwave)
        return pltpu.make_async_remote_copy(
            src_ref=send.at[phase, other],
            dst_ref=recv.at[phase, me_w],
            send_sem=send_sem.at[phase, other],
            recv_sem=recv_sem.at[phase, me_w],
            device_id=(me_s, other),
            device_id_type=MESH,
        )

    def plane_total(phase):
        total = send[phase, me_w]
        for step in range(1, nwave):
            other = lax.rem(me_w + step, nwave)
            pltpu.make_async_remote_copy(
                src_ref=send.at[phase, other],
                dst_ref=recv.at[phase, other],
                send_sem=send_sem.at[phase, other],
                recv_sem=recv_sem.at[phase, other],
                device_id=(me_s, other),
                device_id_type=MESH,
            ).wait_recv()
            total = total + recv[phase, other]
        return total

    def axis_copy(phase):
        group = group_of(phase)
        return pltpu.make_async_remote_copy(
            src_ref=zsend.at[phase],
            dst_ref=zrecv.at[me_s],
            send_sem=zsend_sem.at[phase],
            recv_sem=zrecv_sem.at[me_s],
            device_id=(group, me_w),
            device_id_type=MESH,
        )

    def advance(step, carry):
        phase = lax.div(step, chunk)
        inner = lax.rem(step, chunk)
        evaluate(phase, inner)

        @pl.when(step == chunk)
        def _():
            pl.semaphore_wait(barrier, nwave + nspecies - 2)

        @pl.when(jnp.logical_and(inner == 0, phase > 0))
        def _():
            for other in range(1, nwave):
                plane_copy(phase - 1, other).start()

        @pl.when(jnp.logical_and(inner == chunk - 1, phase > 0))
        def _():
            zsend[phase - 1] = plane_total(phase - 1)
            axis_copy(phase - 1).start()

        return carry

    lax.fori_loop(0, points, advance, 0)
    for step in range(1, nwave):
        plane_copy(last, step).start()
    total = plane_total(last)
    for step in range(1, nspecies):
        other = lax.rem(me_s + step, nspecies)
        pltpu.make_async_remote_copy(
            src_ref=zsend.at[0],
            dst_ref=zrecv.at[other],
            send_sem=zsend_sem.at[0],
            recv_sem=zrecv_sem.at[other],
            device_id=(other, me_w),
            device_id_type=MESH,
        ).wait_recv()
        total = total + zrecv[other]
    for mix in range(mixes):
        for half in range(2):
            out[mix, :, half * LANES : (half + 1) * LANES] = total[:, half * mixes + mix, :]
    for phase in range(nspecies):
        for step in range(1, nwave):
            plane_copy(phase, step).wait_send()
        if phase < last:
            axis_copy(phase).wait_send()


def per_device(
    dest_tiles,
    line_counts,
    wing_widths,
    species_ids,
    offsets,
    strengths,
    doppler,
    lorentz,
    energy,
    temp_scale,
    press_scale,
    inverse_temp,
    abundances,
):
    nspecies = lax.axis_size("species")
    nwave = lax.axis_size("wave")
    nblocks = dest_tiles.shape[1]
    mixes, _, sub, points = abundances.shape
    chunk = points // nspecies
    rows = 2 * mixes
    total_rows = nwave * rows
    lines = nblocks * LANES
    sizes = (nspecies, nwave, nblocks, points, mixes, sub)
    smem = pl.BlockSpec(memory_space=pltpu.SMEM)
    vmem = pl.BlockSpec(memory_space=pltpu.VMEM)
    table = pltpu.VMEM((nblocks, points, LANES), jnp.float32)
    return pl.pallas_call(
        functools.partial(kernel, sizes),
        out_shape=jax.ShapeDtypeStruct((mixes, chunk, 2 * LANES), jnp.float32),
        in_specs=[smem] * 7 + [vmem] * 6,
        out_specs=vmem,
        scratch_shapes=[
            pltpu.VMEM((WINDOW, lines), jnp.float32),
            table,
            table,
            table,
            pltpu.VMEM((nblocks, points * rows, LANES), jnp.float32),
            pltpu.VMEM((nblocks, STAGES, STEP, LANES), jnp.float32),
            pltpu.VMEM((nblocks, 2 * total_rows, LANES), jnp.bfloat16),
            pltpu.VMEM((mixes, sub, points, LANES), jnp.float32),
            pltpu.VMEM((2 * total_rows, 2 * LANES), jnp.float32),
            pltpu.VMEM((total_rows + 2 * rows, LANES), jnp.float32),
            pltpu.VMEM((nspecies, nwave, chunk, rows, LANES), jnp.float32),
            pltpu.VMEM((nspecies, nwave, chunk, rows, LANES), jnp.float32),
            pltpu.VMEM((nspecies, chunk, rows, LANES), jnp.float32),
            pltpu.VMEM((nspecies, chunk, rows, LANES), jnp.float32),
            pltpu.SemaphoreType.DMA((nspecies, nwave)),
            pltpu.SemaphoreType.DMA((nspecies, nwave)),
            pltpu.SemaphoreType.DMA((nspecies,)),
            pltpu.SemaphoreType.DMA((nspecies,)),
        ],
        compiler_params=pltpu.CompilerParams(collective_id=0, has_side_effects=True),
    )(
        dest_tiles.reshape(1, nblocks),
        line_counts,
        wing_widths,
        temp_scale,
        press_scale,
        inverse_temp,
        abundances,
        species_ids,
        offsets,
        strengths,
        doppler,
        lorentz,
        energy,
    )


def solution(mesh):
    lines = P("species", "wave")
    return jax.shard_map(
        per_device,
        mesh=mesh,
        in_specs=(P("species", "wave", None),)
        + (lines,) * 8
        + (P(), P(), P(), P(None, "species", None, None)),
        out_specs=P(None, "species", "wave"),
        check_vma=False,
    )
```

time: 31.3 us -> 29.5 us (0.942)
  Pallas kernels: 29.7 us -> 27.9 us
    pallas_call x1, Pallas kernels: 29.7 us -> 27.9 us  [per_device(): pl.pallas_call(functools.partial(kernel, sizes), out_shape=jax.ShapeDtype...]
where the time goes in v1:
time: 29.5 us; the launch traced here: 29.3 us
  Pallas kernels  27.9 us (95%)
  local copies, waits for them, and re-layouts  1.32 us (4%)
    pallas_call x1, Pallas kernels, per_device(): pl.pallas_call(functools.partial(kernel, sizes), out_shape=jax.ShapeDtype...  27.9 us
    unnamed x1, local copies, waits for them, and re-layouts  1.32 us

profile of v1, /device:TPU:0, one launch (start us, length us, event | category | flops | bytes accessed | tf_op | source)
XLA Modules:
  0.0 29.3 jit_solution(3095398832404756837)
XLA Ops:
  0.0 27.9 %shard_map.127 = f32[4,4,256]{2,1,0:T(4,128)} custom-call(s32[1,32]{1,0:T(1,128)} %bitcast.1, s32[1,32]{1,0:T(1,128)} %counts.1, s32[1,32]{1,0:T(1,128)} %wings.1, f32[16]{0:T(128)} %temp.1, f32[16]{0:T(128)} %press.1, f32[16]{0:T(128)} %inverse.1, f32[4,1,4,16]{3,2,1,0:T(4,128)} %abund.1, s32[1,4096]{1,0:T(1,128)} %kinds.1, f32[1,4096]{1,0:T(1,128)} %offsets.1, ...), custom_call_target="tpu_custom_call" | custom-call | tf_op jit(solution)/shard_map/pallas_call | solution.py:329
  27.9 1.3 %copy.15 = f32[4,4,256]{2,1,0:T(4,128)} copy(f32[4,4,256]{2,1,0:T(4,128)} %shard_map.127) | data formatting | bytes 32768

commit v2 on v1

--- a/solution.py
+++ b/solution.py
@@ -15,6 +15,8 @@
 SPAN = QUARTER + 2 * HALO
 STAGES = 2
 FAR = 1e37
+RATIO = False
+PAIR = 2
 MESH = pl.DeviceIdType.MESH
 
 
@@ -63,8 +65,10 @@
 ):
     nspecies, nwave, nblocks, points, mixes, sub = sizes
     chunk = points // nspecies
+    turns = chunk // PAIR
     last = nspecies - 1
     rows = 2 * mixes
+    tile_rows = 2 * rows
     total_rows = nwave * rows
     me_s = lax.axis_index("species")
     me_w = lax.axis_index("wave")
@@ -91,8 +95,10 @@
     lane_row = lax.broadcasted_iota(jnp.int32, (1, LANES), 1)
     local = lax.broadcasted_iota(jnp.int32, (WINDOW, LANES), 0).astype(jnp.float32) - HALO
     row_point = lax.broadcasted_iota(jnp.int32, (points, LANES), 0)
-    row8 = lax.broadcasted_iota(jnp.int32, (rows, LANES), 0)
-    row_half = lax.div(row8, mixes)
+    row16 = lax.broadcasted_iota(jnp.int32, (2 * rows, LANES), 0)
+    row_quarter = (
+        lax.rem(lax.div(row16, mixes), 2) * 2 + lax.div(row16, rows)
+    ).astype(jnp.float32)
     for mix in range(mixes):
         for kind in range(sub):
             value = jnp.zeros((points, LANES), jnp.float32)
@@ -133,8 +139,13 @@
         ratio = lor * inv
         eta = ratio * (1.36603 + ratio * (-0.47719 + ratio * 0.11116))
         decay[block] = -4.0 * (inv * inv)
-        lor_amp[block] = eta * inv * (4.0 * 0.15915494)
-        gau_amp[block] = (1.0 - eta) * inv * 0.9394373
+        amp_l = eta * inv * (4.0 * 0.15915494)
+        amp_g = (1.0 - eta) * inv * 0.9394373
+        if RATIO:
+            gau_amp[block] = amp_g / amp_l
+        else:
+            lor_amp[block] = amp_l
+            gau_amp[block] = amp_g
         boltz = jnp.exp(-(inverse_col * energy[:, here]))
         strength = jnp.where(lane_row < counts[0, block], strengths[:, here], 0.0)
         kind_row = kinds[:, here]
@@ -143,17 +154,16 @@
             for kind in range(1, sub):
                 mixed = jnp.where(kind_row == kind, coef[mix, kind], mixed)
             mixed = (mixed * strength) * boltz
+            if RATIO:
+                mixed = mixed * amp_l
             for half in range(2):
                 table[block, pl.ds(half * mixes + mix, points, stride=rows), :] = mixed
+        chosen = jnp.where(row_quarter == quarter, 1.0, 0.0)
         target = tiles[0, block]
-        for parity in range(2):
-            chosen = jnp.where((2 * row_half + parity).astype(jnp.float32) == quarter, 1.0, 0.0)
-            for tile in range(0, nwave, 2):
-                pair = jnp.concatenate(
-                    [jnp.where(target == tile, chosen, 0.0), jnp.where(target == tile + 1, chosen, 0.0)],
-                    axis=0,
-                )
-                route[block, pl.ds(parity * total_rows + tile * rows, 2 * rows), :] = pair.astype(jnp.bfloat16)
+        for tile in range(nwave):
+            route[block, tile * tile_rows : (tile + 1) * tile_rows, :] = jnp.where(
+                target == tile, chosen, 0.0
+            ).astype(jnp.bfloat16)
         return carry
 
     lax.fori_loop(0, nblocks, prepare, 0, unroll=4)
@@ -161,24 +171,38 @@
     accum[...] = jnp.zeros(accum.shape, jnp.float32)
     edge[...] = jnp.zeros(edge.shape, jnp.float32)
     low_lane = lax.broadcasted_iota(jnp.int32, (total_rows, LANES), 1) < QUARTER
+    lane_all = lax.broadcasted_iota(jnp.int32, (LANES, 2 * total_rows), 1)
+    odd_lane = lax.rem(lax.div(lane_all, rows), 2) == 1
 
     def group_of(phase):
-        return lax.rem(me_s + 1 + phase, nspecies)
-
-    def evaluate(phase, inner):
-        point = group_of(phase) * chunk + inner
-        weights = []
-        profiles = []
-        for block in range(nblocks):
+        if nspecies % 2:
+            return lax.rem(me_s + 1 + phase, nspecies)
+        pairs = nspecies // 2
+        ahead = pairs - 1 - lax.div(phase, 2)
+        other = lax.rem(me_s + 1 + lax.rem(phase, 2), 2)
+        return lax.rem(lax.div(me_s, 2) + ahead, pairs) * 2 + other
+
+    def evaluate(step):
+        base = group_of(lax.div(step, turns)) * chunk + lax.rem(step, turns) * PAIR
+        spots = range(PAIR)
+        weights = [[] for _ in spots]
+        profiles = [[] for _ in spots]
+
+        def one(slot, block):
+            point = base + slot
             here = pl.ds(block * LANES, LANES)
             slope = jnp.broadcast_to(decay[block, pl.ds(point, 1), :], (STEP, LANES))
-            amp_l = jnp.broadcast_to(lor_amp[block, pl.ds(point, 1), :], (STEP, LANES))
             amp_g = jnp.broadcast_to(gau_amp[block, pl.ds(point, 1), :], (STEP, LANES))
+            if not RATIO:
+                amp_l = jnp.broadcast_to(lor_amp[block, pl.ds(point, 1), :], (STEP, LANES))
             pieces = []
             for piece in range(WINDOW // STEP):
                 sq = square[piece * STEP : (piece + 1) * STEP, here]
                 power = sq * slope
-                value = amp_l / (1.0 - power) + amp_g * jnp.exp2(power)
+                if RATIO:
+                    value = 1.0 / (1.0 - power) + amp_g * jnp.exp2(power)
+                else:
+                    value = amp_l / (1.0 - power) + amp_g * jnp.exp2(power)
                 pieces.append(value.astype(jnp.bfloat16))
             blank = jnp.zeros((STEP, LANES), jnp.bfloat16)
             for stage in range(STAGES):
@@ -187,59 +211,80 @@
                 shifted = [blank] * hop + pieces
                 stay = pieces + [blank] * hop
                 pieces = [jnp.where(on, a, b) for a, b in zip(shifted, stay)]
-            profiles.append(jnp.concatenate(pieces, axis=0))
+            profiles[slot].append(jnp.concatenate(pieces, axis=0))
             weight = table[block, pl.ds(pl.multiple_of(point * rows, rows), rows), :]
             packed = jnp.concatenate([weight, weight], axis=0).astype(jnp.bfloat16)
-            weights.append(
+            weights[slot].append(
                 jnp.concatenate(
                     [
-                        packed * route[block, part * 2 * rows : (part + 1) * 2 * rows, :]
-                        for part in range(nwave)
+                        packed * route[block, tile * tile_rows : (tile + 1) * tile_rows, :]
+                        for tile in range(nwave)
                     ],
                     axis=0,
                 )
             )
-        accum[:, 0:SPAN] = lax.dot_general(
-            jnp.concatenate(weights, axis=1),
-            jnp.concatenate(profiles, axis=1),
-            (((1,), (1,)), ((), ())),
-            preferred_element_type=jnp.float32,
-        )
-        even_a = pltpu.roll(accum[0:total_rows, 0:LANES], QUARTER, 1)
-        even_b = pltpu.roll(accum[0:total_rows, LANES : 2 * LANES], QUARTER, 1)
-        odd_a = accum[total_rows : 2 * total_rows, 0:LANES]
-        odd_b = accum[total_rows : 2 * total_rows, LANES : 2 * LANES]
-        edge[rows : rows + total_rows, :] = jnp.where(low_lane, odd_b, even_a)
-        above = edge[rows - mixes : rows - mixes + total_rows, :]
-        below = edge[rows + mixes : rows + mixes + total_rows, :]
-        joined = (odd_a + jnp.where(low_lane, even_a, even_b)) + jnp.where(low_lane, above, below)
-        for tile in range(nwave):
-            send[phase, tile, inner] = joined[tile * rows : (tile + 1) * rows]
-
-    def plane_copy(phase, step):
+
+        for slot in spots:
+            for block in range(nblocks):
+                one(slot, block)
+            accum[slot] = lax.dot_general(
+                jnp.concatenate(profiles[slot], axis=1),
+                jnp.concatenate(weights[slot], axis=1),
+                (((1,), (1,)), ((), ())),
+                preferred_element_type=jnp.float32,
+            )
+
+    def finish(step):
+        phase = lax.div(step, turns)
+        first = lax.rem(step, turns) * PAIR
+        for slot in range(PAIR):
+            near = jnp.where(odd_lane, accum[slot, 0:LANES, :], accum[slot, QUARTER:SPAN, :]).T
+            far = jnp.concatenate([accum[slot, LANES:SPAN, :], accum[slot, 0:QUARTER, :]], axis=0).T
+
+            def part(array, parity):
+                return jnp.concatenate(
+                    [
+                        array[(2 * tile + parity) * rows : (2 * tile + parity + 1) * rows]
+                        for tile in range(nwave)
+                    ],
+                    axis=0,
+                )
+
+            edge[slot, rows : rows + total_rows, :] = jnp.where(low_lane, part(far, 1), part(far, 0))
+            above = edge[slot, rows - mixes : rows - mixes + total_rows, :]
+            below = edge[slot, rows + mixes : rows + mixes + total_rows, :]
+            joined = (part(near, 0) + part(near, 1)) + jnp.where(low_lane, above, below)
+            for tile in range(nwave):
+                send[phase, tile, first + slot] = joined[tile * rows : (tile + 1) * rows]
+
+    def plane_copy(phase, step, sent=None):
         other = lax.rem(me_w + step, nwave)
+        index = phase if sent is None else last + sent
+        part = pl.ds(0, chunk) if sent is None else pl.ds(sent * PAIR, PAIR)
         return pltpu.make_async_remote_copy(
-            src_ref=send.at[phase, other],
-            dst_ref=recv.at[phase, me_w],
-            send_sem=send_sem.at[phase, other],
-            recv_sem=recv_sem.at[phase, me_w],
+            src_ref=send.at[phase, other, part],
+            dst_ref=recv.at[phase, me_w, part],
+            send_sem=send_sem.at[index, other],
+            recv_sem=recv_sem.at[index, me_w],
             device_id=(me_s, other),
             device_id_type=MESH,
         )
 
-    def plane_total(phase):
-        total = send[phase, me_w]
+    def plane_total(phase, sent=None):
+        index = phase if sent is None else last + sent
+        part = pl.ds(0, chunk) if sent is None else pl.ds(sent * PAIR, PAIR)
+        total = send[phase, me_w, part]
         for step in range(1, nwave):
             other = lax.rem(me_w + step, nwave)
             pltpu.make_async_remote_copy(
-                src_ref=send.at[phase, other],
-                dst_ref=recv.at[phase, other],
-                send_sem=send_sem.at[phase, other],
-                recv_sem=recv_sem.at[phase, other],
+                src_ref=send.at[phase, other, part],
+                dst_ref=recv.at[phase, other, part],
+                send_sem=send_sem.at[index, other],
+                recv_sem=recv_sem.at[index, other],
                 device_id=(me_s, other),
                 device_id_type=MESH,
             ).wait_recv()
-            total = total + recv[phase, other]
+            total = total + recv[phase, other, part]
         return total
 
     def axis_copy(phase):
@@ -253,31 +298,45 @@
             device_id_type=MESH,
         )
 
+    def relay(phase):
+        zsend[phase] = plane_total(phase)
+        axis_copy(phase).start()
+
     def advance(step, carry):
-        phase = lax.div(step, chunk)
-        inner = lax.rem(step, chunk)
-        evaluate(phase, inner)
-
-        @pl.when(step == chunk)
+        finish(jnp.maximum(step - 1, 0))
+        evaluate(step)
+        phase = lax.div(step, turns)
+        turn = lax.rem(step, turns)
+
+        @pl.when(step == turns)
         def _():
             pl.semaphore_wait(barrier, nwave + nspecies - 2)
 
-        @pl.when(jnp.logical_and(inner == 0, phase > 0))
+        @pl.when(jnp.logical_and(turn == 0, phase > 0))
         def _():
             for other in range(1, nwave):
                 plane_copy(phase - 1, other).start()
 
-        @pl.when(jnp.logical_and(inner == chunk - 1, phase > 0))
+        @pl.when(jnp.logical_and(turn == 0, phase > 1))
         def _():
-            zsend[phase - 1] = plane_total(phase - 1)
-            axis_copy(phase - 1).start()
+            relay(phase - 2)
+
+        for sent in range(turns - 1):
+
+            @pl.when(step == last * turns + sent + 1)
+            def _():
+                for other in range(1, nwave):
+                    plane_copy(last, other, sent).start()
 
         return carry
 
-    lax.fori_loop(0, points, advance, 0)
+    lax.fori_loop(0, nspecies * turns, advance, 0)
+    finish(nspecies * turns - 1)
     for step in range(1, nwave):
-        plane_copy(last, step).start()
-    total = plane_total(last)
+        plane_copy(last, step, turns - 1).start()
+    relay(last - 1)
+    parts = [plane_total(last, sent) for sent in range(turns)]
+    total = parts[0] if turns == 1 else jnp.concatenate(parts, axis=0)
     for step in range(1, nspecies):
         other = lax.rem(me_s + step, nspecies)
         pltpu.make_async_remote_copy(
@@ -292,11 +351,13 @@
     for mix in range(mixes):
         for half in range(2):
             out[mix, :, half * LANES : (half + 1) * LANES] = total[:, half * mixes + mix, :]
-    for phase in range(nspecies):
-        for step in range(1, nwave):
+    for step in range(1, nwave):
+        for phase in range(last):
             plane_copy(phase, step).wait_send()
-        if phase < last:
-            axis_copy(phase).wait_send()
+        for sent in range(turns):
+            plane_copy(last, step, sent).wait_send()
+    for phase in range(last):
+        axis_copy(phase).wait_send()
 
 
 def per_device(
@@ -319,6 +380,8 @@
     nblocks = dest_tiles.shape[1]
     mixes, _, sub, points = abundances.shape
     chunk = points // nspecies
+    turns = chunk // PAIR
+    last = nspecies - 1
     rows = 2 * mixes
     total_rows = nwave * rows
     lines = nblocks * LANES
@@ -340,14 +403,14 @@
             pltpu.VMEM((nblocks, STAGES, STEP, LANES), jnp.float32),
             pltpu.VMEM((nblocks, 2 * total_rows, LANES), jnp.bfloat16),
             pltpu.VMEM((mixes, sub, points, LANES), jnp.float32),
-            pltpu.VMEM((2 * total_rows, 2 * LANES), jnp.float32),
-            pltpu.VMEM((total_rows + 2 * rows, LANES), jnp.float32),
+            pltpu.VMEM((PAIR, SPAN, 2 * total_rows), jnp.float32),
+            pltpu.VMEM((PAIR, total_rows + 2 * rows, LANES), jnp.float32),
             pltpu.VMEM((nspecies, nwave, chunk, rows, LANES), jnp.float32),
             pltpu.VMEM((nspecies, nwave, chunk, rows, LANES), jnp.float32),
             pltpu.VMEM((nspecies, chunk, rows, LANES), jnp.float32),
             pltpu.VMEM((nspecies, chunk, rows, LANES), jnp.float32),
-            pltpu.SemaphoreType.DMA((nspecies, nwave)),
-            pltpu.SemaphoreType.DMA((nspecies, nwave)),
+            pltpu.SemaphoreType.DMA((last + turns, nwave)),
+            pltpu.SemaphoreType.DMA((last + turns, nwave)),
             pltpu.SemaphoreType.DMA((nspecies,)),
             pltpu.SemaphoreType.DMA((nspecies,)),
         ],

time: 29.5 us -> 27.5 us (0.932)
  Pallas kernels: 27.9 us -> 25.9 us
    pallas_call x1, Pallas kernels: 27.9 us -> 25.9 us  [per_device(): pl.pallas_call(functools.partial(kernel, sizes), out_shape=jax.ShapeDtype...]
where the time goes in v2:
time: 27.5 us; the launch traced here: 27.2 us
  Pallas kernels  25.9 us (94%)
  local copies, waits for them, and re-layouts  1.32 us (5%)
    pallas_call x1, Pallas kernels, per_device(): pl.pallas_call(functools.partial(kernel, sizes), out_shape=jax.ShapeDtype...  25.9 us
    unnamed x1, local copies, waits for them, and re-layouts  1.32 us

profile of v2, /device:TPU:0, one launch (start us, length us, event | category | flops | bytes accessed | tf_op | source)
XLA Modules:
  0.0 27.2 jit_solution(14240222019966045811)
XLA Ops:
  0.0 25.9 %shard_map.127 = f32[4,4,256]{2,1,0:T(4,128)} custom-call(s32[1,32]{1,0:T(1,128)} %bitcast.1, s32[1,32]{1,0:T(1,128)} %counts.1, s32[1,32]{1,0:T(1,128)} %wings.1, f32[16]{0:T(128)} %temp.1, f32[16]{0:T(128)} %press.1, f32[16]{0:T(128)} %inverse.1, f32[4,1,4,16]{3,2,1,0:T(4,128)} %abund.1, s32[1,4096]{1,0:T(1,128)} %kinds.1, f32[1,4096]{1,0:T(1,128)} %offsets.1, ...), custom_call_target="tpu_custom_call" | custom-call | tf_op jit(solution)/shard_map/pallas_call | solution.py:392
  25.9 1.3 %copy.15 = f32[4,4,256]{2,1,0:T(4,128)} copy(f32[4,4,256]{2,1,0:T(4,128)} %shard_map.127) | data formatting | bytes 32768

commit v3 on v2

--- a/solution.py
+++ b/solution.py
@@ -30,40 +30,46 @@
 
 def kernel(
     sizes,
-    tiles,
-    counts,
-    wings,
-    temp,
-    press,
-    inverse,
-    abund,
-    kinds,
-    offsets,
-    strengths,
-    doppler,
-    lorentz,
-    energy,
-    out,
-    square,
-    decay,
-    lor_amp,
-    gau_amp,
-    table,
-    bits,
-    route,
-    coef,
-    accum,
-    edge,
-    send,
-    recv,
-    zsend,
-    zrecv,
-    send_sem,
-    recv_sem,
-    zsend_sem,
-    zrecv_sem,
+    *refs,
 ):
     nspecies, nwave, nblocks, points, mixes, sub = sizes
+    sources, out, scratch = refs[:13], refs[13], refs[14:]
+    inputs, input_sem = scratch[:13], scratch[13]
+    (
+        tiles,
+        counts,
+        wings,
+        temp,
+        press,
+        inverse,
+        abund,
+        kinds,
+        offsets,
+        strengths,
+        doppler,
+        lorentz,
+        energy,
+    ) = inputs
+    (
+        square,
+        decay,
+        lor_amp,
+        gau_amp,
+        table,
+        bits,
+        route,
+        coef,
+        accum,
+        edge,
+        send,
+        recv,
+        zsend,
+        zrecv,
+        send_sem,
+        recv_sem,
+        zsend_sem,
+        zrecv_sem,
+    ) = scratch[14:]
     chunk = points // nspecies
     turns = chunk // PAIR
     last = nspecies - 1
@@ -73,6 +79,12 @@
     me_s = lax.axis_index("species")
     me_w = lax.axis_index("wave")
 
+    loads = [
+        pltpu.make_async_copy(source, target, input_sem.at[index])
+        for index, (source, target) in enumerate(zip(sources, inputs))
+    ]
+    for load in loads:
+        load.start()
     barrier = pltpu.get_barrier_semaphore()
     for step in range(1, nwave):
         pl.semaphore_signal(
@@ -89,6 +101,8 @@
             device_id_type=MESH,
         )
 
+    for load in loads:
+        load.wait()
     temp_col = column(temp, points)
     press_col = column(press, points)
     inverse_col = column(inverse, points)
@@ -234,8 +248,7 @@
                 preferred_element_type=jnp.float32,
             )
 
-    def finish(step):
-        phase = lax.div(step, turns)
+    def finish(step, phase):
         first = lax.rem(step, turns) * PAIR
         for slot in range(PAIR):
             near = jnp.where(odd_lane, accum[slot, 0:LANES, :], accum[slot, QUARTER:SPAN, :]).T
@@ -303,7 +316,8 @@
         axis_copy(phase).start()
 
     def advance(step, carry):
-        finish(jnp.maximum(step - 1, 0))
+        before = jnp.maximum(step - 1, 0)
+        finish(before, jnp.where(step == last * turns, nspecies, lax.div(before, turns)))
         evaluate(step)
         phase = lax.div(step, turns)
         turn = lax.rem(step, turns)
@@ -312,10 +326,16 @@
         def _():
             pl.semaphore_wait(barrier, nwave + nspecies - 2)
 
-        @pl.when(jnp.logical_and(turn == 0, phase > 0))
+        @pl.when(jnp.logical_and(turn == 0, jnp.logical_and(phase > 0, phase < last)))
         def _():
             for other in range(1, nwave):
                 plane_copy(phase - 1, other).start()
+
+        @pl.when(step == last * turns - 1)
+        def _():
+            finish(step, last - 1)
+            for other in range(1, nwave):
+                plane_copy(last - 1, other).start()
 
         @pl.when(jnp.logical_and(turn == 0, phase > 1))
         def _():
@@ -331,7 +351,7 @@
         return carry
 
     lax.fori_loop(0, nspecies * turns, advance, 0)
-    finish(nspecies * turns - 1)
+    finish(nspecies * turns - 1, last)
     for step in range(1, nwave):
         plane_copy(last, step, turns - 1).start()
     relay(last - 1)
@@ -386,36 +406,7 @@
     total_rows = nwave * rows
     lines = nblocks * LANES
     sizes = (nspecies, nwave, nblocks, points, mixes, sub)
-    smem = pl.BlockSpec(memory_space=pltpu.SMEM)
-    vmem = pl.BlockSpec(memory_space=pltpu.VMEM)
-    table = pltpu.VMEM((nblocks, points, LANES), jnp.float32)
-    return pl.pallas_call(
-        functools.partial(kernel, sizes),
-        out_shape=jax.ShapeDtypeStruct((mixes, chunk, 2 * LANES), jnp.float32),
-        in_specs=[smem] * 7 + [vmem] * 6,
-        out_specs=vmem,
-        scratch_shapes=[
-            pltpu.VMEM((WINDOW, lines), jnp.float32),
-            table,
-            table,
-            table,
-            pltpu.VMEM((nblocks, points * rows, LANES), jnp.float32),
-            pltpu.VMEM((nblocks, STAGES, STEP, LANES), jnp.float32),
-            pltpu.VMEM((nblocks, 2 * total_rows, LANES), jnp.bfloat16),
-            pltpu.VMEM((mixes, sub, points, LANES), jnp.float32),
-            pltpu.VMEM((PAIR, SPAN, 2 * total_rows), jnp.float32),
-            pltpu.VMEM((PAIR, total_rows + 2 * rows, LANES), jnp.float32),
-            pltpu.VMEM((nspecies, nwave, chunk, rows, LANES), jnp.float32),
-            pltpu.VMEM((nspecies, nwave, chunk, rows, LANES), jnp.float32),
-            pltpu.VMEM((nspecies, chunk, rows, LANES), jnp.float32),
-            pltpu.VMEM((nspecies, chunk, rows, LANES), jnp.float32),
-            pltpu.SemaphoreType.DMA((last + turns, nwave)),
-            pltpu.SemaphoreType.DMA((last + turns, nwave)),
-            pltpu.SemaphoreType.DMA((nspecies,)),
-            pltpu.SemaphoreType.DMA((nspecies,)),
-        ],
-        compiler_params=pltpu.CompilerParams(collective_id=0, has_side_effects=True),
-    )(
+    operands = (
         dest_tiles.reshape(1, nblocks),
         line_counts,
         wing_widths,
@@ -430,6 +421,38 @@
         lorentz,
         energy,
     )
+    operands = tuple(pltpu.with_memory_space_constraint(array, pltpu.HBM) for array in operands)
+    spaces = [pltpu.SMEM] * 7 + [pltpu.VMEM] * 6
+    table = pltpu.VMEM((nblocks, points, LANES), jnp.float32)
+    return pl.pallas_call(
+        functools.partial(kernel, sizes),
+        out_shape=jax.ShapeDtypeStruct((mixes, chunk, 2 * LANES), jnp.float32),
+        in_specs=[pl.BlockSpec(memory_space=pltpu.HBM)] * len(operands),
+        out_specs=pl.BlockSpec(memory_space=pltpu.VMEM),
+        scratch_shapes=[space(array.shape, array.dtype) for space, array in zip(spaces, operands)]
+        + [
+            pltpu.SemaphoreType.DMA((len(operands),)),
+            pltpu.VMEM((WINDOW, lines), jnp.float32),
+            table,
+            table,
+            table,
+            pltpu.VMEM((nblocks, points * rows, LANES), jnp.float32),
+            pltpu.VMEM((nblocks, STAGES, STEP, LANES), jnp.float32),
+            pltpu.VMEM((nblocks, 2 * total_rows, LANES), jnp.bfloat16),
+            pltpu.VMEM((mixes, sub, points, LANES), jnp.float32),
+            pltpu.VMEM((PAIR, SPAN, 2 * total_rows), jnp.float32),
+            pltpu.VMEM((PAIR, total_rows + 2 * rows, LANES), jnp.float32),
+            pltpu.VMEM((nspecies + 1, nwave, chunk, rows, LANES), jnp.float32),
+            pltpu.VMEM((nspecies, nwave, chunk, rows, LANES), jnp.float32),
+            pltpu.VMEM((nspecies, chunk, rows, LANES), jnp.float32),
+            pltpu.VMEM((nspecies, chunk, rows, LANES), jnp.float32),
+            pltpu.SemaphoreType.DMA((last + turns, nwave)),
+            pltpu.SemaphoreType.DMA((last + turns, nwave)),
+            pltpu.SemaphoreType.DMA((nspecies,)),
+            pltpu.SemaphoreType.DMA((nspecies,)),
+        ],
+        compiler_params=pltpu.CompilerParams(collective_id=0, has_side_effects=True, vmem_limit_bytes=24 << 20),
+    )(*operands)
 
 
 def solution(mesh):

time: 27.5 us -> 25.1 us (0.913)
  Pallas kernels: 25.9 us -> 24.3 us
  local copies, waits for them, and re-layouts: 1.32 us -> 0.61 us
    pallas_call x1, Pallas kernels: 25.9 us -> 24.3 us  [per_device(): pl.pallas_call(functools.partial(kernel, sizes), out_shape=jax.ShapeDtype...]
    unnamed x1, local copies, waits for them, and re-layouts: 1.32 us -> 0.61 us
where the time goes in v3:
time: 25.1 us; the launch traced here: 24.9 us
  Pallas kernels  24.3 us (97%)
  local copies, waits for them, and re-layouts  0.61 us (2%)
    pallas_call x1, Pallas kernels, per_device(): pl.pallas_call(functools.partial(kernel, sizes), out_shape=jax.ShapeDtype...  24.3 us
    unnamed x1, local copies, waits for them, and re-layouts  0.61 us

profile of v3, /device:TPU:0, one launch (start us, length us, event | category | flops | bytes accessed | tf_op | source)
XLA Modules:
  0.0 24.9 jit_solution(9976624011153884415)
XLA Ops:
  0.0 24.3 %shard_map.127 = f32[4,4,256]{2,1,0:T(4,128)S(1)} custom-call(s32[1,32]{1,0:T(1,128)} %bitcast.1, s32[1,32]{1,0:T(1,128)} %refs_1_.1, s32[1,32]{1,0:T(1,128)} %refs_2_.1, f32[16]{0:T(128)} %refs_3_.1, f32[16]{0:T(128)} %refs_4_.1, f32[16]{0:T(128)} %refs_5_.1, f32[4,1,4,16]{3,2,1,0:T(4,128)} %refs_6_.1, s32[1,4096]{1,0:T(1,128)} %refs_7_.1, ...), custom_call_target="tpu_custom_call" | custom-call | tf_op jit(solution)/shard_map/pallas_call | solution.py:427
  24.3 0.6 %copy.15 = f32[4,4,256]{2,1,0:T(4,128)} copy(f32[4,4,256]{2,1,0:T(4,128)S(1)} %shard_map.127) | data formatting | bytes 32768

commit v4 on v3

--- a/solution.py
+++ b/solution.py
@@ -15,8 +15,6 @@
 SPAN = QUARTER + 2 * HALO
 STAGES = 2
 FAR = 1e37
-RATIO = False
-PAIR = 2
 MESH = pl.DeviceIdType.MESH
 
 
@@ -71,7 +69,6 @@
         zrecv_sem,
     ) = scratch[14:]
     chunk = points // nspecies
-    turns = chunk // PAIR
     last = nspecies - 1
     rows = 2 * mixes
     tile_rows = 2 * rows
@@ -127,7 +124,7 @@
         center = center - quarter * float(QUARTER)
         hop = jnp.clip(jnp.floor(center * (1.0 / STEP)), 0.0, float(QUARTER // STEP - 1))
         reach = wings[0, block].astype(jnp.float32)
-        offset = (local + hop * float(STEP)) - center
+        offset = local - (center - hop * float(STEP))
         sq = offset * offset
         square[:, here] = jnp.where(sq <= reach * reach, sq, FAR)
         hop_int = hop.astype(jnp.int32)
@@ -155,11 +152,8 @@
         decay[block] = -4.0 * (inv * inv)
         amp_l = eta * inv * (4.0 * 0.15915494)
         amp_g = (1.0 - eta) * inv * 0.9394373
-        if RATIO:
-            gau_amp[block] = amp_g / amp_l
-        else:
-            lor_amp[block] = amp_l
-            gau_amp[block] = amp_g
+        lor_amp[block] = amp_l
+        gau_amp[block] = amp_g
         boltz = jnp.exp(-(inverse_col * energy[:, here]))
         strength = jnp.where(lane_row < counts[0, block], strengths[:, here], 0.0)
         kind_row = kinds[:, here]
@@ -168,16 +162,15 @@
             for kind in range(1, sub):
                 mixed = jnp.where(kind_row == kind, coef[mix, kind], mixed)
             mixed = (mixed * strength) * boltz
-            if RATIO:
-                mixed = mixed * amp_l
             for half in range(2):
                 table[block, pl.ds(half * mixes + mix, points, stride=rows), :] = mixed
-        chosen = jnp.where(row_quarter == quarter, 1.0, 0.0)
+        chosen = jnp.where(row_quarter == quarter, 1.0, 0.0).astype(jnp.bfloat16)
+        blank16 = jnp.zeros_like(chosen)
         target = tiles[0, block]
         for tile in range(nwave):
             route[block, tile * tile_rows : (tile + 1) * tile_rows, :] = jnp.where(
-                target == tile, chosen, 0.0
-            ).astype(jnp.bfloat16)
+                target == tile, chosen, blank16
+            )
         return carry
 
     lax.fori_loop(0, nblocks, prepare, 0, unroll=4)
@@ -196,9 +189,9 @@
         other = lax.rem(me_s + 1 + lax.rem(phase, 2), 2)
         return lax.rem(lax.div(me_s, 2) + ahead, pairs) * 2 + other
 
-    def evaluate(step):
-        base = group_of(lax.div(step, turns)) * chunk + lax.rem(step, turns) * PAIR
-        spots = range(PAIR)
+    def evaluate(phase):
+        base = group_of(phase) * chunk
+        spots = range(chunk)
         weights = [[] for _ in spots]
         profiles = [[] for _ in spots]
 
@@ -207,16 +200,12 @@
             here = pl.ds(block * LANES, LANES)
             slope = jnp.broadcast_to(decay[block, pl.ds(point, 1), :], (STEP, LANES))
             amp_g = jnp.broadcast_to(gau_amp[block, pl.ds(point, 1), :], (STEP, LANES))
-            if not RATIO:
-                amp_l = jnp.broadcast_to(lor_amp[block, pl.ds(point, 1), :], (STEP, LANES))
+            amp_l = jnp.broadcast_to(lor_amp[block, pl.ds(point, 1), :], (STEP, LANES))
             pieces = []
             for piece in range(WINDOW // STEP):
                 sq = square[piece * STEP : (piece + 1) * STEP, here]
                 power = sq * slope
-                if RATIO:
-                    value = 1.0 / (1.0 - power) + amp_g * jnp.exp2(power)
-                else:
-                    value = amp_l / (1.0 - power) + amp_g * jnp.exp2(power)
+                value = amp_l / (1.0 - power) + amp_g * jnp.exp2(power)
                 pieces.append(value.astype(jnp.bfloat16))
             blank = jnp.zeros((STEP, LANES), jnp.bfloat16)
             for stage in range(STAGES):
@@ -248,9 +237,8 @@
                 preferred_element_type=jnp.float32,
             )
 
-    def finish(step, phase):
-        first = lax.rem(step, turns) * PAIR
-        for slot in range(PAIR):
+    def finish(phase):
+        for slot in range(chunk):
             near = jnp.where(odd_lane, accum[slot, 0:LANES, :], accum[slot, QUARTER:SPAN, :]).T
             far = jnp.concatenate([accum[slot, LANES:SPAN, :], accum[slot, 0:QUARTER, :]], axis=0).T
 
@@ -268,36 +256,32 @@
             below = edge[slot, rows + mixes : rows + mixes + total_rows, :]
             joined = (part(near, 0) + part(near, 1)) + jnp.where(low_lane, above, below)
             for tile in range(nwave):
-                send[phase, tile, first + slot] = joined[tile * rows : (tile + 1) * rows]
-
-    def plane_copy(phase, step, sent=None):
+                send[phase, tile, slot] = joined[tile * rows : (tile + 1) * rows]
+
+    def plane_copy(phase, step):
         other = lax.rem(me_w + step, nwave)
-        index = phase if sent is None else last + sent
-        part = pl.ds(0, chunk) if sent is None else pl.ds(sent * PAIR, PAIR)
         return pltpu.make_async_remote_copy(
-            src_ref=send.at[phase, other, part],
-            dst_ref=recv.at[phase, me_w, part],
-            send_sem=send_sem.at[index, other],
-            recv_sem=recv_sem.at[index, me_w],
+            src_ref=send.at[phase, other],
+            dst_ref=recv.at[phase, me_w],
+            send_sem=send_sem.at[phase, other],
+            recv_sem=recv_sem.at[phase, me_w],
             device_id=(me_s, other),
             device_id_type=MESH,
         )
 
-    def plane_total(phase, sent=None):
-        index = phase if sent is None else last + sent
-        part = pl.ds(0, chunk) if sent is None else pl.ds(sent * PAIR, PAIR)
-        total = send[phase, me_w, part]
+    def plane_total(phase):
+        total = send[phase, me_w]
         for step in range(1, nwave):
             other = lax.rem(me_w + step, nwave)
             pltpu.make_async_remote_copy(
-                src_ref=send.at[phase, other, part],
-                dst_ref=recv.at[phase, other, part],
-                send_sem=send_sem.at[index, other],
-                recv_sem=recv_sem.at[index, other],
+                src_ref=send.at[phase, other],
+                dst_ref=recv.at[phase, other],
+                send_sem=send_sem.at[phase, other],
+                recv_sem=recv_sem.at[phase, other],
                 device_id=(me_s, other),
                 device_id_type=MESH,
             ).wait_recv()
-            total = total + recv[phase, other, part]
+            total = total + recv[phase, other]
         return total
 
     def axis_copy(phase):
@@ -315,48 +299,40 @@
         zsend[phase] = plane_total(phase)
         axis_copy(phase).start()
 
-    def advance(step, carry):
-        before = jnp.maximum(step - 1, 0)
-        finish(before, jnp.where(step == last * turns, nspecies, lax.div(before, turns)))
-        evaluate(step)
-        phase = lax.div(step, turns)
-        turn = lax.rem(step, turns)
-
-        @pl.when(step == turns)
+    def spread(phase):
+        for step in range(1, nwave):
+            plane_copy(phase, step).start()
+
+    def advance(phase, carry):
+        ready = jnp.logical_and(phase > 0, phase < last)
+        finish(jnp.where(ready, phase - 1, nspecies))
+        evaluate(phase)
+
+        @pl.when(phase == 1)
         def _():
             pl.semaphore_wait(barrier, nwave + nspecies - 2)
 
-        @pl.when(jnp.logical_and(turn == 0, jnp.logical_and(phase > 0, phase < last)))
+        @pl.when(ready)
         def _():
-            for other in range(1, nwave):
-                plane_copy(phase - 1, other).start()
-
-        @pl.when(step == last * turns - 1)
+            spread(phase - 1)
+
+        @pl.when(phase == last - 1)
         def _():
-            finish(step, last - 1)
-            for other in range(1, nwave):
-                plane_copy(last - 1, other).start()
-
-        @pl.when(jnp.logical_and(turn == 0, phase > 1))
+            finish(phase)
+            spread(phase)
+
+        @pl.when(jnp.logical_and(phase > 1, phase < last))
         def _():
             relay(phase - 2)
 
-        for sent in range(turns - 1):
-
-            @pl.when(step == last * turns + sent + 1)
-            def _():
-                for other in range(1, nwave):
-                    plane_copy(last, other, sent).start()
-
         return carry
 
-    lax.fori_loop(0, nspecies * turns, advance, 0)
-    finish(nspecies * turns - 1, last)
-    for step in range(1, nwave):
-        plane_copy(last, step, turns - 1).start()
+    lax.fori_loop(0, nspecies, advance, 0)
+    finish(last)
+    spread(last)
+    relay(last - 2)
     relay(last - 1)
-    parts = [plane_total(last, sent) for sent in range(turns)]
-    total = parts[0] if turns == 1 else jnp.concatenate(parts, axis=0)
+    total = plane_total(last)
     for step in range(1, nspecies):
         other = lax.rem(me_s + step, nspecies)
         pltpu.make_async_remote_copy(
@@ -371,11 +347,9 @@
     for mix in range(mixes):
         for half in range(2):
             out[mix, :, half * LANES : (half + 1) * LANES] = total[:, half * mixes + mix, :]
-    for step in range(1, nwave):
-        for phase in range(last):
+    for phase in range(nspecies):
+        for step in range(1, nwave):
             plane_copy(phase, step).wait_send()
-        for sent in range(turns):
-            plane_copy(last, step, sent).wait_send()
     for phase in range(last):
         axis_copy(phase).wait_send()
 
@@ -400,8 +374,6 @@
     nblocks = dest_tiles.shape[1]
     mixes, _, sub, points = abundances.shape
     chunk = points // nspecies
-    turns = chunk // PAIR
-    last = nspecies - 1
     rows = 2 * mixes
     total_rows = nwave * rows
     lines = nblocks * LANES
@@ -440,14 +412,14 @@
             pltpu.VMEM((nblocks, STAGES, STEP, LANES), jnp.float32),
             pltpu.VMEM((nblocks, 2 * total_rows, LANES), jnp.bfloat16),
             pltpu.VMEM((mixes, sub, points, LANES), jnp.float32),
-            pltpu.VMEM((PAIR, SPAN, 2 * total_rows), jnp.float32),
-            pltpu.VMEM((PAIR, total_rows + 2 * rows, LANES), jnp.float32),
+            pltpu.VMEM((chunk, SPAN, 2 * total_rows), jnp.float32),
+            pltpu.VMEM((chunk, total_rows + 2 * rows, LANES), jnp.float32),
             pltpu.VMEM((nspecies + 1, nwave, chunk, rows, LANES), jnp.float32),
             pltpu.VMEM((nspecies, nwave, chunk, rows, LANES), jnp.float32),
             pltpu.VMEM((nspecies, chunk, rows, LANES), jnp.float32),
             pltpu.VMEM((nspecies, chunk, rows, LANES), jnp.float32),
-            pltpu.SemaphoreType.DMA((last + turns, nwave)),
-            pltpu.SemaphoreType.DMA((last + turns, nwave)),
+            pltpu.SemaphoreType.DMA((nspecies, nwave)),
+            pltpu.SemaphoreType.DMA((nspecies, nwave)),
             pltpu.SemaphoreType.DMA((nspecies,)),
             pltpu.SemaphoreType.DMA((nspecies,)),
         ],

time: 25.1 us -> 24.7 us (0.984)
  Pallas kernels: 24.3 us -> 23.9 us
    pallas_call x1, Pallas kernels: 24.3 us -> 23.9 us  [per_device(): pl.pallas_call(functools.partial(kernel, sizes), out_shape=jax.ShapeDtype...]
where the time goes in v4:
time: 24.7 us; the launch traced here: 24.5 us
  Pallas kernels  23.9 us (97%)
  local copies, waits for them, and re-layouts  0.61 us (2%)
    pallas_call x1, Pallas kernels, per_device(): pl.pallas_call(functools.partial(kernel, sizes), out_shape=jax.ShapeDtype...  23.9 us
    unnamed x1, local copies, waits for them, and re-layouts  0.61 us

profile of v4, /device:TPU:0, one launch (start us, length us, event | category | flops | bytes accessed | tf_op | source)
XLA Modules:
  0.0 24.5 jit_solution(5547311754616747443)
XLA Ops:
  0.0 23.9 %shard_map.127 = f32[4,4,256]{2,1,0:T(4,128)S(1)} custom-call(s32[1,32]{1,0:T(1,128)} %bitcast.1, s32[1,32]{1,0:T(1,128)} %refs_1_.1, s32[1,32]{1,0:T(1,128)} %refs_2_.1, f32[16]{0:T(128)} %refs_3_.1, f32[16]{0:T(128)} %refs_4_.1, f32[16]{0:T(128)} %refs_5_.1, f32[4,1,4,16]{3,2,1,0:T(4,128)} %refs_6_.1, s32[1,4096]{1,0:T(1,128)} %refs_7_.1, ...), custom_call_target="tpu_custom_call" | custom-call | tf_op jit(solution)/shard_map/pallas_call | solution.py:399
  23.9 0.6 %copy.15 = f32[4,4,256]{2,1,0:T(4,128)} copy(f32[4,4,256]{2,1,0:T(4,128)S(1)} %shard_map.127) | data formatting | bytes 32768

commit v5 on v4

--- a/solution.py
+++ b/solution.py
@@ -51,7 +51,6 @@
     (
         square,
         decay,
-        lor_amp,
         gau_amp,
         table,
         bits,
@@ -152,8 +151,7 @@
         decay[block] = -4.0 * (inv * inv)
         amp_l = eta * inv * (4.0 * 0.15915494)
         amp_g = (1.0 - eta) * inv * 0.9394373
-        lor_amp[block] = amp_l
-        gau_amp[block] = amp_g
+        gau_amp[block] = amp_g / amp_l
         boltz = jnp.exp(-(inverse_col * energy[:, here]))
         strength = jnp.where(lane_row < counts[0, block], strengths[:, here], 0.0)
         kind_row = kinds[:, here]
@@ -162,6 +160,7 @@
             for kind in range(1, sub):
                 mixed = jnp.where(kind_row == kind, coef[mix, kind], mixed)
             mixed = (mixed * strength) * boltz
+            mixed = mixed * amp_l
             for half in range(2):
                 table[block, pl.ds(half * mixes + mix, points, stride=rows), :] = mixed
         chosen = jnp.where(row_quarter == quarter, 1.0, 0.0).astype(jnp.bfloat16)
@@ -200,12 +199,11 @@
             here = pl.ds(block * LANES, LANES)
             slope = jnp.broadcast_to(decay[block, pl.ds(point, 1), :], (STEP, LANES))
             amp_g = jnp.broadcast_to(gau_amp[block, pl.ds(point, 1), :], (STEP, LANES))
-            amp_l = jnp.broadcast_to(lor_amp[block, pl.ds(point, 1), :], (STEP, LANES))
             pieces = []
             for piece in range(WINDOW // STEP):
                 sq = square[piece * STEP : (piece + 1) * STEP, here]
                 power = sq * slope
-                value = amp_l / (1.0 - power) + amp_g * jnp.exp2(power)
+                value = 1.0 / (1.0 - power) + amp_g * jnp.exp2(power)
                 pieces.append(value.astype(jnp.bfloat16))
             blank = jnp.zeros((STEP, LANES), jnp.bfloat16)
             for stage in range(STAGES):
@@ -407,7 +405,6 @@
             pltpu.VMEM((WINDOW, lines), jnp.float32),
             table,
             table,
-            table,
             pltpu.VMEM((nblocks, points * rows, LANES), jnp.float32),
             pltpu.VMEM((nblocks, STAGES, STEP, LANES), jnp.float32),
             pltpu.VMEM((nblocks, 2 * total_rows, LANES), jnp.bfloat16),

time: 24.7 us -> 23.7 us (0.960)
  Pallas kernels: 23.9 us -> 22.9 us
    pallas_call x1, Pallas kernels: 23.9 us -> 22.9 us  [per_device(): pl.pallas_call(functools.partial(kernel, sizes), out_shape=jax.ShapeDtype...]
where the time goes in v5:
time: 23.7 us; the launch traced here: 23.5 us
  Pallas kernels  22.9 us (97%)
  local copies, waits for them, and re-layouts  0.61 us (3%)
    pallas_call x1, Pallas kernels, per_device(): pl.pallas_call(functools.partial(kernel, sizes), out_shape=jax.ShapeDtype...  22.9 us
    unnamed x1, local copies, waits for them, and re-layouts  0.61 us

profile of v5, /device:TPU:0, one launch (start us, length us, event | category | flops | bytes accessed | tf_op | source)
XLA Modules:
  0.0 23.5 jit_solution(16448102665166375386)
XLA Ops:
  0.0 22.9 %shard_map.127 = f32[4,4,256]{2,1,0:T(4,128)S(1)} custom-call(s32[1,32]{1,0:T(1,128)} %bitcast.1, s32[1,32]{1,0:T(1,128)} %refs_1_.1, s32[1,32]{1,0:T(1,128)} %refs_2_.1, f32[16]{0:T(128)} %refs_3_.1, f32[16]{0:T(128)} %refs_4_.1, f32[16]{0:T(128)} %refs_5_.1, f32[4,1,4,16]{3,2,1,0:T(4,128)} %refs_6_.1, s32[1,4096]{1,0:T(1,128)} %refs_7_.1, ...), custom_call_target="tpu_custom_call" | custom-call | tf_op jit(solution)/shard_map/pallas_call | solution.py:397
  22.9 0.6 %copy.15 = f32[4,4,256]{2,1,0:T(4,128)} copy(f32[4,4,256]{2,1,0:T(4,128)S(1)} %shard_map.127) | data formatting | bytes 32768

commit v6 on v5

--- a/solution.py
+++ b/solution.py
@@ -163,13 +163,12 @@
             mixed = mixed * amp_l
             for half in range(2):
                 table[block, pl.ds(half * mixes + mix, points, stride=rows), :] = mixed
-        chosen = jnp.where(row_quarter == quarter, 1.0, 0.0).astype(jnp.bfloat16)
-        blank16 = jnp.zeros_like(chosen)
+        chosen = jnp.where(row_quarter == quarter, 1.0, 0.0)
         target = tiles[0, block]
         for tile in range(nwave):
             route[block, tile * tile_rows : (tile + 1) * tile_rows, :] = jnp.where(
-                target == tile, chosen, blank16
-            )
+                target == tile, chosen, 0.0
+            ).astype(jnp.bfloat16)
         return carry
 
     lax.fori_loop(0, nblocks, prepare, 0, unroll=4)
@@ -302,34 +301,22 @@
             plane_copy(phase, step).start()
 
     def advance(phase, carry):
-        ready = jnp.logical_and(phase > 0, phase < last)
-        finish(jnp.where(ready, phase - 1, nspecies))
         evaluate(phase)
-
-        @pl.when(phase == 1)
+        finish(phase)
+
+        @pl.when(phase == 0)
         def _():
             pl.semaphore_wait(barrier, nwave + nspecies - 2)
 
-        @pl.when(ready)
+        spread(phase)
+
+        @pl.when(phase > 0)
         def _():
-            spread(phase - 1)
-
-        @pl.when(phase == last - 1)
-        def _():
-            finish(phase)
-            spread(phase)
-
-        @pl.when(jnp.logical_and(phase > 1, phase < last))
-        def _():
-            relay(phase - 2)
+            relay(phase - 1)
 
         return carry
 
     lax.fori_loop(0, nspecies, advance, 0)
-    finish(last)
-    spread(last)
-    relay(last - 2)
-    relay(last - 1)
     total = plane_total(last)
     for step in range(1, nspecies):
         other = lax.rem(me_s + step, nspecies)
@@ -411,7 +398,7 @@
             pltpu.VMEM((mixes, sub, points, LANES), jnp.float32),
             pltpu.VMEM((chunk, SPAN, 2 * total_rows), jnp.float32),
             pltpu.VMEM((chunk, total_rows + 2 * rows, LANES), jnp.float32),
-            pltpu.VMEM((nspecies + 1, nwave, chunk, rows, LANES), jnp.float32),
+            pltpu.VMEM((nspecies, nwave, chunk, rows, LANES), jnp.float32),
             pltpu.VMEM((nspecies, nwave, chunk, rows, LANES), jnp.float32),
             pltpu.VMEM((nspecies, chunk, rows, LANES), jnp.float32),
             pltpu.VMEM((nspecies, chunk, rows, LANES), jnp.float32),

time: 23.7 us -> 22.6 us (0.954)
  Pallas kernels: 22.9 us -> 21.8 us
    pallas_call x1, Pallas kernels: 22.9 us -> 21.8 us  [per_device(): pl.pallas_call(functools.partial(kernel, sizes), out_shape=jax.ShapeDtype...]
where the time goes in v6:
time: 22.6 us; the launch traced here: 22.4 us
  Pallas kernels  21.8 us (96%)
  local copies, waits for them, and re-layouts  0.61 us (3%)
    pallas_call x1, Pallas kernels, per_device(): pl.pallas_call(functools.partial(kernel, sizes), out_shape=jax.ShapeDtype...  21.8 us
    unnamed x1, local copies, waits for them, and re-layouts  0.61 us

profile of v6, /device:TPU:0, one launch (start us, length us, event | category | flops | bytes accessed | tf_op | source)
XLA Modules:
  0.0 22.4 jit_solution(13000151248237819447)
XLA Ops:
  0.0 21.8 %shard_map.127 = f32[4,4,256]{2,1,0:T(4,128)S(1)} custom-call(s32[1,32]{1,0:T(1,128)} %bitcast.1, s32[1,32]{1,0:T(1,128)} %refs_1_.1, s32[1,32]{1,0:T(1,128)} %refs_2_.1, f32[16]{0:T(128)} %refs_3_.1, f32[16]{0:T(128)} %refs_4_.1, f32[16]{0:T(128)} %refs_5_.1, f32[4,1,4,16]{3,2,1,0:T(4,128)} %refs_6_.1, s32[1,4096]{1,0:T(1,128)} %refs_7_.1, ...), custom_call_target="tpu_custom_call" | custom-call | tf_op jit(solution)/shard_map/pallas_call | solution.py:384
  21.8 0.6 %copy.15 = f32[4,4,256]{2,1,0:T(4,128)} copy(f32[4,4,256]{2,1,0:T(4,128)S(1)} %shard_map.127) | data formatting | bytes 32768

commit v7 on v6

--- a/solution.py
+++ b/solution.py
@@ -51,6 +51,7 @@
     (
         square,
         decay,
+        lor_amp,
         gau_amp,
         table,
         bits,
@@ -151,7 +152,8 @@
         decay[block] = -4.0 * (inv * inv)
         amp_l = eta * inv * (4.0 * 0.15915494)
         amp_g = (1.0 - eta) * inv * 0.9394373
-        gau_amp[block] = amp_g / amp_l
+        lor_amp[block] = amp_l
+        gau_amp[block] = amp_g
         boltz = jnp.exp(-(inverse_col * energy[:, here]))
         strength = jnp.where(lane_row < counts[0, block], strengths[:, here], 0.0)
         kind_row = kinds[:, here]
@@ -160,7 +162,6 @@
             for kind in range(1, sub):
                 mixed = jnp.where(kind_row == kind, coef[mix, kind], mixed)
             mixed = (mixed * strength) * boltz
-            mixed = mixed * amp_l
             for half in range(2):
                 table[block, pl.ds(half * mixes + mix, points, stride=rows), :] = mixed
         chosen = jnp.where(row_quarter == quarter, 1.0, 0.0)
@@ -198,11 +199,12 @@
             here = pl.ds(block * LANES, LANES)
             slope = jnp.broadcast_to(decay[block, pl.ds(point, 1), :], (STEP, LANES))
             amp_g = jnp.broadcast_to(gau_amp[block, pl.ds(point, 1), :], (STEP, LANES))
+            amp_l = jnp.broadcast_to(lor_amp[block, pl.ds(point, 1), :], (STEP, LANES))
             pieces = []
             for piece in range(WINDOW // STEP):
                 sq = square[piece * STEP : (piece + 1) * STEP, here]
                 power = sq * slope
-                value = 1.0 / (1.0 - power) + amp_g * jnp.exp2(power)
+                value = amp_l / (1.0 - power) + amp_g * jnp.exp2(power)
                 pieces.append(value.astype(jnp.bfloat16))
             blank = jnp.zeros((STEP, LANES), jnp.bfloat16)
             for stage in range(STAGES):
@@ -392,6 +394,7 @@
             pltpu.VMEM((WINDOW, lines), jnp.float32),
             table,
             table,
+            table,
             pltpu.VMEM((nblocks, points * rows, LANES), jnp.float32),
             pltpu.VMEM((nblocks, STAGES, STEP, LANES), jnp.float32),
             pltpu.VMEM((nblocks, 2 * total_rows, LANES), jnp.bfloat16),

time: 22.6 us -> 23.7 us (1.049)
  Pallas kernels: 21.8 us -> 22.9 us
    pallas_call x1, Pallas kernels: 21.8 us -> 22.9 us  [per_device(): pl.pallas_call(functools.partial(kernel, sizes), out_shape=jax.ShapeDtype...]
where the time goes in v7:
time: 23.7 us; the launch traced here: 23.5 us
  Pallas kernels  22.9 us (97%)
  local copies, waits for them, and re-layouts  0.61 us (3%)
    pallas_call x1, Pallas kernels, per_device(): pl.pallas_call(functools.partial(kernel, sizes), out_shape=jax.ShapeDtype...  22.9 us
    unnamed x1, local copies, waits for them, and re-layouts  0.61 us

profile of v7, /device:TPU:0, one launch (start us, length us, event | category | flops | bytes accessed | tf_op | source)
XLA Modules:
  0.0 23.5 jit_solution(5131687403971099127)
XLA Ops:
  0.0 22.9 %shard_map.127 = f32[4,4,256]{2,1,0:T(4,128)S(1)} custom-call(s32[1,32]{1,0:T(1,128)} %bitcast.1, s32[1,32]{1,0:T(1,128)} %refs_1_.1, s32[1,32]{1,0:T(1,128)} %refs_2_.1, f32[16]{0:T(128)} %refs_3_.1, f32[16]{0:T(128)} %refs_4_.1, f32[16]{0:T(128)} %refs_5_.1, f32[4,1,4,16]{3,2,1,0:T(4,128)} %refs_6_.1, s32[1,4096]{1,0:T(1,128)} %refs_7_.1, ...), custom_call_target="tpu_custom_call" | custom-call | tf_op jit(solution)/shard_map/pallas_call | solution.py:386
  22.9 0.6 %copy.15 = f32[4,4,256]{2,1,0:T(4,128)} copy(f32[4,4,256]{2,1,0:T(4,128)S(1)} %shard_map.127) | data formatting | bytes 32768

commit v8 on v6

--- a/solution.py
+++ b/solution.py
@@ -97,7 +97,8 @@
             device_id_type=MESH,
         )
 
-    for load in loads:
+    edge[...] = jnp.zeros(edge.shape, jnp.float32)
+    for load in loads[:7]:
         load.wait()
     temp_col = column(temp, points)
     press_col = column(press, points)
@@ -115,6 +116,9 @@
             for point in range(points):
                 value = jnp.where(row_point == point, abund[mix, 0, kind, point], value)
             coef[mix, kind] = value
+
+    for load in loads[7:]:
+        load.wait()
 
     def prepare(block, carry):
         here = pl.ds(pl.multiple_of(block * LANES, LANES), LANES)
@@ -173,8 +177,6 @@
 
     lax.fori_loop(0, nblocks, prepare, 0, unroll=4)
 
-    accum[...] = jnp.zeros(accum.shape, jnp.float32)
-    edge[...] = jnp.zeros(edge.shape, jnp.float32)
     low_lane = lax.broadcasted_iota(jnp.int32, (total_rows, LANES), 1) < QUARTER
     lane_all = lax.broadcasted_iota(jnp.int32, (LANES, 2 * total_rows), 1)
     odd_lane = lax.rem(lax.div(lane_all, rows), 2) == 1

time: 22.6 us -> 22.6 us (level)
  no operation moved by 1% of the time
where the time goes in v8:
time: 22.6 us; the launch traced here: 22.4 us
  Pallas kernels  21.8 us (96%)
  local copies, waits for them, and re-layouts  0.61 us (3%)
    pallas_call x1, Pallas kernels, per_device(): pl.pallas_call(functools.partial(kernel, sizes), out_shape=jax.ShapeDtype...  21.8 us
    unnamed x1, local copies, waits for them, and re-layouts  0.61 us

profile of v8, /device:TPU:0, one launch (start us, length us, event | category | flops | bytes accessed | tf_op | source)
XLA Modules:
  0.0 22.4 jit_solution(211585279805331689)
XLA Ops:
  0.0 21.8 %shard_map.127 = f32[4,4,256]{2,1,0:T(4,128)S(1)} custom-call(s32[1,32]{1,0:T(1,128)} %bitcast.1, s32[1,32]{1,0:T(1,128)} %refs_1_.1, s32[1,32]{1,0:T(1,128)} %refs_2_.1, f32[16]{0:T(128)} %refs_3_.1, f32[16]{0:T(128)} %refs_4_.1, f32[16]{0:T(128)} %refs_5_.1, f32[4,1,4,16]{3,2,1,0:T(4,128)} %refs_6_.1, s32[1,4096]{1,0:T(1,128)} %refs_7_.1, ...), custom_call_target="tpu_custom_call" | custom-call | tf_op jit(solution)/shard_map/pallas_call | solution.py:386
  21.8 0.6 %copy.15 = f32[4,4,256]{2,1,0:T(4,128)} copy(f32[4,4,256]{2,1,0:T(4,128)S(1)} %shard_map.127) | data formatting | bytes 32768
